TPU v7x, 256 devices: a whole 4x4x8 slice. The times are simulated.
256 devices in a mesh: tile: 4 (over y), proj: 16 (over x, z_hi, core), cuts: 4 (over z_lo).
Axes of the slice: x: 4, y: 4, z: 8 (z_hi: 2, z_lo: 4; z = z_hi * 4 + z_lo), core: 2. Of those that a mesh axis runs over, the one named last changes fastest.
Arguments:
- object_field: float32 [64, 2, 384, 2048], P(('proj', 'cuts'), None, None, 'tile'), may hold values from -5 to 5
- probe_field: float32 [2, 256, 256], replicated, may hold values from -6 to 6
- amplitudes: bfloat16 [64, 4, 6, 256, 256], P(('proj', 'cuts'), 'tile'), may hold values from 0 to 16
- pos_rows: int32 [64, 4, 6], P(('proj', 'cuts'), 'tile'), may hold values from 0 to 128
- pos_cols: int32 [64, 4, 6], P(('proj', 'cuts'), 'tile'), may hold values from 0 to 512
- counts: int32 [64, 4], P(('proj', 'cuts'), 'tile'), may hold values from 1 to 6, as said below
- admm_dual: float32 [64, 32, 2048], P(('proj', 'cuts'), None, 'tile'), may hold values from -4 to 4
- volume: float32 [32, 2048, 2048], P('cuts', ('tile', 'proj')), may hold values from -6 to 6
- proj_weights: bfloat16 [16, 2048, 2048], P(None, ('tile', 'proj')), may hold values from -0.125 to 0.125
- ray_weights: float32 [16, 2048], replicated, may hold values from -0.125 to 0.125
- angle_ids: int32 [64], replicated, may hold values from 0 to 15
Outputs:
- new_object: float32 [64, 2, 384, 2048], P(('proj', 'cuts'), None, None, 'tile')
- new_probe: float32 [2, 256, 256], replicated
- new_volume: float32 [32, 2048, 2048], P('cuts', ('tile', 'proj'))
Inputs may be any that keep to these rules, and one draw needn't show every extreme that they name: `counts`: every tile holds at least one live position and at most 6; exactly one tile of one projection holds 6, every other holds at most 3.
All inputs are finite; a program needn't handle non-finite values.
Results may differ from a plain program's by a relative error of at most 0.00095.
The roundings to bfloat16 on the way count: a program that leaves them out, or rounds other values in their place, can miss the bound.
Values may be sent and summed in bfloat16 or wider, within the bound.
A program may use at most 64 MiB of HBM per device.

v0:
```python
import math
import jax
import jax.numpy as jnp
from jax import lax
from jax.sharding import PartitionSpec as P

PB = 256
tomo_step = 1.0


def shifted(value, axis, steps):
    count = lax.axis_size(axis)
    leading, last = (max(0, -steps), min(count, count - steps))
    return lax.ppermute(value, axis, [(source, source + steps) for source in range(leading, last)])


def dft_tables(side):
    indices = jnp.arange(side, dtype=jnp.int32)
    products = indices[:, None] * indices[None, :] % side
    phase_angle = products.astype(jnp.float32) * (2.0 * math.pi / side)
    norm_factor = 1.0 / math.sqrt(side)
    return (
        (jnp.cos(phase_angle) * norm_factor).astype(jnp.bfloat16),
        (-jnp.sin(phase_angle) * norm_factor).astype(jnp.bfloat16),
    )


def matmul(left, right):
    return jnp.dot(left, right, preferred_element_type=jnp.float32)


def complex_matmul(left_real, left_imag, right_real, right_imag):
    out_real = matmul(left_real, right_real) - matmul(left_imag, right_imag)
    out_imag = matmul(left_real, right_imag) + matmul(left_imag, right_real)
    return (out_real, out_imag)


def patch_terms(patch_real, patch_imag, probe_real, probe_imag, amplitude, dft_real, dft_imag):
    wave_real = (probe_real * patch_real - probe_imag * patch_imag).astype(jnp.bfloat16)
    wave_imag = (probe_real * patch_imag + probe_imag * patch_real).astype(jnp.bfloat16)
    half_real, half_imag = complex_matmul(dft_real, dft_imag, wave_real, wave_imag)
    half_real = half_real.astype(jnp.bfloat16)
    half_imag = half_imag.astype(jnp.bfloat16)
    far_real, far_imag = complex_matmul(half_real, half_imag, dft_real, dft_imag)
    modulus = jnp.sqrt(far_real * far_real + far_imag * far_imag + 0.25)
    factor = amplitude.astype(jnp.float32) / modulus - 1.0
    diff_real = (far_real * factor).astype(jnp.bfloat16)
    diff_imag = (far_imag * factor).astype(jnp.bfloat16)
    conj_imag = -dft_imag
    back_half_real, back_half_imag = complex_matmul(dft_real, conj_imag, diff_real, diff_imag)
    back_half_real = back_half_real.astype(jnp.bfloat16)
    back_half_imag = back_half_imag.astype(jnp.bfloat16)
    back_real, back_imag = complex_matmul(back_half_real, back_half_imag, dft_real, conj_imag)
    object_real = probe_real * back_real + probe_imag * back_imag
    object_imag = probe_real * back_imag - probe_imag * back_real
    probe_grad_real = patch_real * back_real + patch_imag * back_imag
    probe_grad_imag = patch_real * back_imag - patch_imag * back_real
    energy = jnp.mean(patch_real * patch_real + patch_imag * patch_imag)
    return (
        jnp.stack([object_real, object_imag]),
        jnp.stack([probe_grad_real, probe_grad_imag]),
        energy,
    )


def tile_edges(values, offset):
    return shifted(values, "tile", offset)


def on_device(
    object_field,
    probe_field,
    amplitudes,
    pos_rows,
    pos_cols,
    counts,
    admm_dual,
    volume,
    proj_weights,
    ray_weights,
    angle_ids,
):
    half_side = PB // 2
    own_object = object_field[0]
    tile_cols = own_object.shape[2]
    from_left = tile_edges(own_object[:, :, tile_cols - half_side :], 1)
    from_right = tile_edges(own_object[:, :, :half_side], -1)
    extended = jnp.concatenate([from_left, own_object, from_right], axis=2)
    dft_real, dft_imag = dft_tables(PB)
    probe_real = probe_field[0]
    probe_imag = probe_field[1]
    zero_index = jnp.zeros((), jnp.int32)
    live_count = counts[0, 0]
    slot_total = amplitudes.shape[2]

    def slot_step(slot_index, state_tuple, weight):
        grad_sum, probe_sum, energy_sum = state_tuple
        anchor = (zero_index, pos_rows[0, 0, slot_index], pos_cols[0, 0, slot_index])
        object_patch = lax.dynamic_slice(extended, anchor, (2, PB, PB))
        object_part, probe_part, energy = patch_terms(
            object_patch[0],
            object_patch[1],
            probe_real,
            probe_imag,
            amplitudes[0, 0, slot_index],
            dft_real,
            dft_imag,
        )
        current = lax.dynamic_slice(grad_sum, anchor, (2, PB, PB))
        grad_sum = lax.dynamic_update_slice(grad_sum, current + weight * object_part, anchor)
        return (grad_sum, probe_sum + weight * probe_part, energy_sum + weight * energy)

    running = (
        jnp.zeros(extended.shape, jnp.float32),
        jnp.zeros((2, PB, PB), jnp.float32),
        jnp.zeros((), jnp.float32),
    )
    running = lax.fori_loop(
        0,
        slot_total,
        lambda slot_index, state_tuple: slot_step(
            slot_index, state_tuple, (slot_index < live_count).astype(jnp.float32)
        ),
        running,
    )
    grad_sum, probe_sum, energy_sum = running
    to_right_edge = tile_edges(grad_sum[:, :, :half_side], -1)
    to_left_edge = tile_edges(grad_sum[:, :, tile_cols + half_side :], 1)
    own_cells = grad_sum[:, :, half_side : half_side + tile_cols]
    own_cells = own_cells.at[:, :, :half_side].add(to_left_edge)
    own_cells = own_cells.at[:, :, tile_cols - half_side :].add(to_right_edge)
    probe_flat = jnp.concatenate([probe_sum.reshape(-1), jnp.broadcast_to(energy_sum, (128,))])
    probe_flat = lax.psum(probe_flat, ("tile", "proj", "cuts"))
    probe_grad = probe_flat[: probe_sum.size].reshape(probe_sum.shape)
    energy = probe_flat[probe_sum.size]
    new_probe = probe_field + probe_grad / (energy + 1e-05)
    probe_peak = jnp.max(probe_real * probe_real + probe_imag * probe_imag)
    new_object = (own_object + own_cells / (probe_peak + 1e-05))[None]
    slab_total = admm_dual.shape[1]
    first_row = (own_object.shape[1] - slab_total) // 2
    slab_values = new_object[:, 1, first_row : first_row + slab_total, :] + admm_dual
    arrived = lax.all_to_all(
        lax.all_to_all(slab_values, "proj", split_axis=2, concat_axis=0, tiled=True),
        "cuts",
        split_axis=1,
        concat_axis=0,
        tiled=True,
    )
    proj_count = lax.axis_size("proj")
    cuts_count = lax.axis_size("cuts")
    slab_dev = arrived.shape[1]
    u_share = arrived.shape[2]
    projections = proj_count * cuts_count
    arrived = arrived.reshape(cuts_count, proj_count, slab_dev, u_share).transpose(1, 0, 2, 3)
    target = (
        arrived.reshape(projections, slab_dev, u_share)
        .transpose(2, 0, 1)
        .reshape(u_share, projections * slab_dev)
    )
    angle_count = ray_weights.shape[0]
    x_share = volume.shape[1]
    width = volume.shape[2]
    onehot = (angle_ids[:, None] == jnp.arange(angle_count, dtype=jnp.int32)[None, :]).astype(
        jnp.float32
    )
    ray_table = jnp.dot(
        onehot, ray_weights, precision=lax.Precision.HIGHEST, preferred_element_type=jnp.float32
    )
    ray_sums = jnp.einsum("zxy,ay->azx", volume, ray_table, precision=lax.Precision.HIGHEST).astype(
        jnp.bfloat16
    )
    spread = onehot.astype(jnp.bfloat16)[:, :, None, None] * ray_sums[:, None, :, :]
    spread = spread.transpose(1, 3, 0, 2).reshape(angle_count * x_share, projections * slab_dev)
    weight_flat = proj_weights.reshape(angle_count * x_share, width)
    partial_term = lax.dot_general(
        weight_flat, spread, (((0,), (0,)), ((), ())), preferred_element_type=jnp.float32
    )
    own_rows = lax.psum_scatter(partial_term, ("tile", "proj"), scatter_dimension=0, tiled=True)
    own_residue = (own_rows - target).astype(jnp.bfloat16)
    residue = lax.all_gather(own_residue, ("tile", "proj"), axis=0, tiled=True)
    backproj = matmul(weight_flat, residue)
    backproj = backproj.reshape(angle_count, x_share, projections, slab_dev)
    back_sums = jnp.einsum("gxaz,ag->azx", backproj, onehot, precision=lax.Precision.HIGHEST)
    gradient = jnp.einsum("azx,ay->zxy", back_sums, ray_table, precision=lax.Precision.HIGHEST)
    new_volume = volume - tomo_step * gradient
    return (new_object, new_probe, new_volume)


def solution(mesh):
    in_specs = (
        P(("proj", "cuts"), None, None, "tile"),
        P(),
        P(("proj", "cuts"), "tile", None, None, None),
        P(("proj", "cuts"), "tile", None),
        P(("proj", "cuts"), "tile", None),
        P(("proj", "cuts"), "tile"),
        P(("proj", "cuts"), None, "tile"),
        P("cuts", ("tile", "proj"), None),
        P(None, ("tile", "proj"), None),
        P(),
        P(),
    )
    out_specs = (P(("proj", "cuts"), None, None, "tile"), P(), P("cuts", ("tile", "proj"), None))
    return jax.shard_map(
        on_device, mesh=mesh, in_specs=in_specs, out_specs=out_specs, check_vma=False
    )
```

profile of v0, /device:TPU:1, one launch (start us, length us, event | category | flops | bytes accessed | tf_op | source)
XLA Modules:
  0.0 628.5 jit_solution(16933225154168796481)
XLA Ops:
  8.1 3.2 copy.17
  13.5 4.0 collective-permute-start
  23.7 3.4 mul.431
  27.1 3.3 convolution_bitcast_fusion
  30.4 5.3 copy.31
  37.5 3.2 pad_maximum_fusion
  42.3 245.5 %while.23 = (s32[]{:T(128)}, f32[2,384,768]{1,2,0:T(8,128)}, f32[2,256,256]{2,1,0:T(8,128)}, f32[]{:T(128)}, s32[1,1,6]{2,1,0:T(1,128)S(1)}, /*index=5*/s32[1,1,...) while((s32[]{:T(128)}, f32[2,384,768]{1,2,0:T(8,128)}, ...), condition=%wide.region_2.3_spmd.clone.clone, body=%wide.region_0.2_spmd.clone.clone.sunk | while | flops 558956544 | bytes 21102956 | solution.py:118
  68.0 3.0 fusion.228
  75.4 6.6 %dynamic_update_slice.13 = f32[2,384,768]{1,2,0:T(8,128)} dynamic-update-slice(f32[2,384,768]{1,2,0:T(8,128)} %get-tuple-element.644, f32[2,256,256]{1,2,0:T(8,128)S(1)} %copy.50, s32[]{:T(128)} %constant.167.clone.1..sunk, s32[]{:T(128)S(6)} %select_n.153, s32[]{:T(128)S(6)} %select_n.154) | dynamic-update-slice | bytes 1048580 | tf_op jit(solution)/shard_map/while/body/eval_jaxpr/dynamic_update_slice | solution.py:110
  116.7 6.0 dynamic_update_slice.13
  157.4 6.2 dynamic_update_slice.13
  198.3 6.3 dynamic_update_slice.13
  239.3 6.6 %dynamic_update_slice.13 = f32[2,384,768]{1,2,0:T(8,128)} dynamic-update-slice(f32[2,384,768]{1,2,0:T(8,128)} %get-tuple-element.644, f32[2,256,256]{1,2,0:T(8,128)S(1)} %copy.50, s32[]{:T(128)} %constant.167.clone.1..sunk, s32[]{:T(128)S(6)} %select_n.153, s32[]{:T(128)S(6)} %select_n.154) | dynamic-update-slice | bytes 1048580 | tf_op jit(solution)/shard_map/while/body/eval_jaxpr/dynamic_update_slice | solution.py:110
  280.6 6.3 %dynamic_update_slice.13 = f32[2,384,768]{1,2,0:T(8,128)} dynamic-update-slice(f32[2,384,768]{1,2,0:T(8,128)} %get-tuple-element.644, f32[2,256,256]{1,2,0:T(8,128)S(1)} %copy.50, s32[]{:T(128)} %constant.167.clone.1..sunk, s32[]{:T(128)S(6)} %select_n.153, s32[]{:T(128)S(6)} %select_n.154) | dynamic-update-slice | bytes 1048580 | tf_op jit(solution)/shard_map/while/body/eval_jaxpr/dynamic_update_slice | solution.py:110
  289.7 5.9 collective-permute-start.2
  303.9 3.2 collective-permute-done.3
  313.5 22.6 %all_to_all.27 = f32[16,1,1024]{2,1,0:T(1,128)S(1)} all-to-all(f32[16,1,1024]{2,1,0:T(1,128)S(1)} %reshape.139), channel_id=1, replica_groups=mesh['tile'=4,'proj'=16,'cuts'=4] {'proj'}, dimensions={0} | all-to-all | bytes 131072 | tf_op jit(solution)/shard_map/all_to_all | solution.py:143
  340.0 3.3 all-to-all-start.1
  344.5 3.3 all-to-all-done.1
  348.8 102.0 %reduce-scatter.4.cloned.1.call-done = f32[32,512]{1,0:T(8,128)} async-done(((f32[2048,512]{1,0:T(8,128)}), f32[32,512]{1,0:T(8,128)}) %reduce-scatter.4.cloned.1.call-update) | async-done | bytes 65552
  452.6 145.6 %all-reduce.3.cloned.1.call-done = f32[131200]{0:T(1024)} async-done(((f32[131200]{0:T(1024)}), f32[131200]{0:T(1024)}) %all-reduce.3.cloned.1.call-update) | async-done | bytes 524816 | tf_op jit(solution)/shard_map/psum | solution.py:133
  604.0 3.0 copy.28
  612.4 3.8 fusion.126
  616.4 4.7 convolution_subtract_fusion.4
  (237 shorter events, 220.2 us)
Async XLA Ops:
  8.0 19.1 %copy-start = (bf16[16,32,2048]{2,1,0:T(8,128)(2,1)S(1)}, bf16[16,32,2048]{2,1,0:T(8,128)(2,1)}, u32[]{:S(2)}) copy-start(bf16[16,32,2048]{2,1,0:T(8,128)(2,1)} %param.25) | copy-start | bytes 6291460
  8.0 10.8 %copy-start.13 = (s32[64]{0:T(128)S(1)}, s32[64]{0:T(128)}, u32[]{:S(2)}) copy-start(s32[64]{0:T(128)} %param.27) | copy-start | bytes 772
  8.0 10.9 %copy-start.9 = (f32[16,2048]{1,0:T(8,128)S(1)}, f32[16,2048]{1,0:T(8,128)}, u32[]{:S(2)}) copy-start(f32[16,2048]{1,0:T(8,128)} %param.26) | copy-start | bytes 393220
  8.0 442.8 %reduce-scatter.4.cloned.1.call-start = ((), (), s32[]{:S(2)}) async-start(), calls=%async_computation.5 | async-start | bytes 4259840
  11.2 8.9 %copy-start.3 = (f32[8,32,2048]{2,1,0:T(8,128)S(1)}, f32[8,32,2048]{2,1,0:T(8,128)}, u32[]{:S(2)}) copy-start(f32[8,32,2048]{2,1,0:T(8,128)} %param.24) | copy-start | bytes 6291460
  13.5 24.0 %collective-permute-start = (f32[2,384,128]{1,2,0:T(8,128)}, f32[2,384,128]{1,2,0:T(8,128)S(1)}, u32[]{:S(2)}, u32[]{:S(2)}) collective-permute-start(f32[2,384,128]{1,2,0:T(8,128)} %get-tuple-element.528), channel_id=1, source_target_pairs={{0,64},{64,128},{128,192},{1,65},{65,129},{129,193},{2,66},{66,130... | collective-permute-start | bytes 1179656 | tf_op jit(solution)/shard_map/ppermute | solution.py:14
  17.6 19.9 %collective-permute-start.1 = (f32[2,384,128]{1,2,0:T(8,128)}, f32[2,384,128]{1,2,0:T(8,128)}, u32[]{:S(2)}, u32[]{:S(2)}) collective-permute-start(f32[2,384,128]{1,2,0:T(8,128)} %get-tuple-element.529), channel_id=1, source_target_pairs={{64,0},{128,64},{192,128},{65,1},{129,65},{193,129},{66,2},{130,66... | collective-permute-start | bytes 1179656 | tf_op jit(solution)/shard_map/ppermute | solution.py:14
  19.4 0.8 copy-start.7
  35.7 1.0 copy-start.5
  40.7 1.6 copy-start.11
  40.7 1.6 copy-start.12
  42.2 254.7 %copy-start.10 = (f32[1,32,512]{2,1,0:T(8,128)S(1)}, f32[1,32,512]{2,1,0:T(8,128)}, u32[]{:S(2)}) copy-start(f32[1,32,512]{2,1,0:T(8,128)} %param.23) | copy-start | bytes 196612
  287.7 9.4 %copy-start.6 = (f32[2,256,256]{2,1,0:T(8,128)S(1)}, f32[2,256,256]{2,1,0:T(8,128)}, u32[]{:S(2)}) copy-start(f32[2,256,256]{2,1,0:T(8,128)} %param.18) | copy-start | bytes 1572868
  289.7 13.1 %collective-permute-start.2 = (f32[2,384,128]{1,2,0:T(8,128)}, f32[2,384,128]{1,2,0:T(8,128)}, u32[]{:S(2)}, u32[]{:S(2)}) collective-permute-start(f32[2,384,128]{1,2,0:T(8,128)} %get-tuple-element.527), channel_id=1, source_target_pairs={{0,64},{64,128},{128,192},{1,65},{65,129},{129,193},{2,66},{66,130... | collective-permute-start | bytes 1179656 | tf_op jit(solution)/shard_map/ppermute | solution.py:14
  295.7 11.4 %collective-permute-start.3 = (f32[2,384,128]{1,2,0:T(8,128)S(1)}, f32[2,384,128]{1,2,0:T(8,128)}, u32[]{:S(2)}, u32[]{:S(2)}) collective-permute-start(f32[2,384,128]{1,2,0:T(8,128)S(1)} %get-tuple-element.526), channel_id=1, source_target_pairs={{64,0},{128,64},{192,128},{65,1},{129,65},{193,129},{66,2},{130,66... | collective-permute-start | bytes 1179656 | tf_op jit(solution)/shard_map/ppermute | solution.py:14
  298.4 9.8 %copy-start.1 = (f32[1,2,384,512]{2,3,1,0:T(8,128)S(1)}, f32[1,2,384,512]{2,3,1,0:T(8,128)}, u32[]{:S(2)}) copy-start(f32[1,2,384,512]{2,3,1,0:T(8,128)} %copy.17) | copy-start | bytes 4718596
  308.4 1.1 copy-start.4
  309.5 33.8 %copy-start.2 = (f32[2,256,256]{2,1,0:T(8,128)S(1)}, f32[2,256,256]{2,1,0:T(8,128)}, u32[]{:S(2)}) copy-start(f32[2,256,256]{2,1,0:T(8,128)} %get-tuple-element.383) | copy-start | bytes 1572868
  340.0 7.9 %all-to-all-start.1 = ((f32[4,1,4096]{2,1,0:T(1,128)}), f32[4,1,4096]{2,1,0:T(1,128)S(1)}, u32[]{:S(2)}, u32[]{:S(2)}) async-start(f32[4,1,4096]{2,1,0:T(1,128)} %reshape.141), calls=%async_computation.1 | async-start | bytes 131072 | tf_op jit(solution)/shard_map/all_to_all | solution.py:142
  343.3 254.9 %all-reduce.3.cloned.1.call-start = ((), (), s32[]{:S(2)}) async-start(), calls=%async_computation.3 | async-start | bytes 1056768 | tf_op jit(solution)/shard_map/psum | solution.py:133
  344.5 262.5 %all-gather.2.cloned.1.call-start = ((), (), s32[]{:S(2)}) async-start(), calls=%async_computation.4 | async-start | bytes 2129920 | tf_op jit(solution)/shard_map/all_gather | solution.py:180
  612.4 4.0 copy-start.8
Sparse Core Ops, SparseCore 0:
  35.8 414.9 reduce-scatter.3
  454.3 86.0 all-gather.1
Sparse Core Ops, SparseCore 1:
  349.8 248.3 all-reduce.2
where the time goes:
time: 632 us; the launch traced here: 629 us
  waiting for transfers between devices  257 us (41%)
  matrix products  143 us (23%)
  local copies, waits for them, and re-layouts  99.8 us (16%)
  other arithmetic  42.6 us (7%)
  loops' own time  30.5 us (5%)
  blocking collectives  22.6 us (4%)
  between operations  17.1 us (3%)
  starting transfers between devices  16 us (3%)
    psum x1, waiting for transfers between devices, on_device(): probe_flat = lax.psum(probe_flat, ('tile', 'proj', 'cuts'))  146 us
    dot_general x97, matrix products, matmul(): return jnp.dot(left, right, preferred_element_type=jnp.float32)  129 us
    unnamed x4, waiting for transfers between devices  102 us
    dynamic_update_slice x12, local copies, waits for them, and re-layouts, slot_step(): lax.dynamic_update_slice(grad_sum, current + weight * object_part, anchor)  39.1 us
    another operation x1, loops' own time, on_device(): lax.fori_loop(0, slot_total, lambda slot_index, state_tuple: slot_step(sl...  30.5 us
    all_to_all x1, blocking collectives, on_device(): lax.all_to_all(slab_values, 'proj', split_axis=2, concat_axis=0, tiled=True)  22.6 us
    unnamed x40, local copies, waits for them, and re-layouts  18.8 us
  transfers between devices with their start and end apart: 8, of which 5 were waited for; matrix products, arithmetic and copies ran while one was open for 42% of the time, Pallas kernels for 0%

commit v1 on v0

--- a/solution.py
+++ b/solution.py
@@ -6,6 +6,10 @@
 
 PB = 256
 tomo_step = 1.0
+balance_thing = lambda arr: jnp.concatenate(
+    lax.all_to_all(jnp.stack(jnp.split(arr, lax.axis_size("proj"), axis=2), axis=0), "proj", 0, 0),
+    axis=0,
+)
 
 
 def shifted(value, axis, steps):
@@ -140,11 +144,7 @@
     first_row = (own_object.shape[1] - slab_total) // 2
     slab_values = new_object[:, 1, first_row : first_row + slab_total, :] + admm_dual
     arrived = lax.all_to_all(
-        lax.all_to_all(slab_values, "proj", split_axis=2, concat_axis=0, tiled=True),
-        "cuts",
-        split_axis=1,
-        concat_axis=0,
-        tiled=True,
+        balance_thing(slab_values), "cuts", split_axis=1, concat_axis=0, tiled=True
     )
     proj_count = lax.axis_size("proj")
     cuts_count = lax.axis_size("cuts")

time: 632 us -> 610 us (0.965)
  local copies, waits for them, and re-layouts: 99.8 us -> 74.5 us
  matrix products: 143 us -> 150 us
    unnamed x4, waiting for transfers between devices: 102 us -> 122 us
    psum x1, waiting for transfers between devices: 146 us -> 128 us  [on_device(): probe_flat = lax.psum(probe_flat, ('tile', 'proj', 'cuts'))]
    add x6 -> x1, other arithmetic: 10.4 us -> 0.01 us  [on_device(): new_object[:, 1, first_row:first_row + slab_total, :] + admm_dual]
    add x6, other arithmetic: 6.61 us -> 15.1 us  [slot_step(): current + weight * object_part]
    slice x7 -> x0, local copies, waits for them, and re-layouts: 8.17 us -> none  [the longest x6 8.04 us: slot_step(): object_patch[0]]
    unnamed x40 -> x48, local copies, waits for them, and re-layouts: 18.8 us -> 11.6 us
    dynamic_update_slice x12 -> x6, local copies, waits for them, and re-layouts: 39.1 us -> 37.5 us  [slot_step(): lax.dynamic_update_slice(grad_sum, current + weight * object_part, anchor)]
  transfers between devices with their start and end apart: 8 -> 8, of which waited for: 5 -> 5; matrix products, arithmetic and copies ran while one was open for 42% -> 40% of each run, Pallas kernels for 0% -> 0%
where the time goes in v1:
time: 610 us; the launch traced here: 607 us
  waiting for transfers between devices  258 us (42%)
  matrix products  150 us (25%)
  local copies, waits for them, and re-layouts  74.5 us (12%)
  other arithmetic  36.4 us (6%)
  loops' own time  32.1 us (5%)
  blocking collectives  24.8 us (4%)
  between operations  17.1 us (3%)
  starting transfers between devices  14.5 us (2%)
    dot_general x97, matrix products, matmul(): return jnp.dot(left, right, preferred_element_type=jnp.float32)  135 us
    psum x1, waiting for transfers between devices, on_device(): probe_flat = lax.psum(probe_flat, ('tile', 'proj', 'cuts'))  128 us
    unnamed x4, waiting for transfers between devices  122 us
    dynamic_update_slice x6, local copies, waits for them, and re-layouts, slot_step(): lax.dynamic_update_slice(grad_sum, current + weight * object_part, anchor)  37.5 us
    another operation x1, loops' own time, on_device(): lax.fori_loop(0, slot_total, lambda slot_index, state_tuple: slot_step(sl...  32.1 us
    all_to_all x1, blocking collectives, lax.all_to_all(jnp.stack(jnp.split(arr, lax.axis_size('proj'), axis=2), a...  24.8 us
    add x6, other arithmetic, slot_step(): current + weight * object_part  15.1 us
  transfers between devices with their start and end apart: 8, of which 5 were waited for; matrix products, arithmetic and copies ran while one was open for 40% of the time, Pallas kernels for 0%

profile of v1, /device:TPU:1, one launch (start us, length us, event | category | flops | bytes accessed | tf_op | source)
XLA Modules:
  0.0 606.9 jit_solution(2859612051960517087)
XLA Ops:
  11.6 5.4 collective-permute-start
  23.4 3.4 mul.431
  26.8 3.3 convolution_bitcast_fusion
  30.1 5.3 copy.57
  41.2 231.7 %while.23 = (s32[]{:T(128)}, f32[2,384,768]{2,1,0:T(8,128)}, f32[2,256,256]{2,1,0:T(8,128)}, f32[]{:T(128)}, s32[1,1,6]{2,1,0:T(1,128)S(1)}, /*index=5*/s32[1,1,...) while((s32[]{:T(128)}, f32[2,384,768]{2,1,0:T(8,128)}, ...), condition=%wide.region_2.3_spmd.clone.clone, body=%wide.region_0.2_spmd.clone.clone.sunk | while | flops 558956544 | bytes 15860098 | solution.py:122
  65.8 3.9 add_bitcast_fusion.4
  72.8 6.4 %dynamic_update_slice.13 = f32[2,384,768]{2,1,0:T(8,128)} dynamic-update-slice(f32[2,384,768]{2,1,0:T(8,128)} %get-tuple-element.624, f32[2,256,256]{2,1,0:T(8,128)S(1)} %get-tuple-element.602, s32[]{:T(128)} %constant.167.clone.1..sunk, s32[]{:T(128)S(6)} %select_n.153, s32[]{:T(128)S(6)} %select_n.154) | dynamic-update-slice | bytes 1048580 | tf_op jit(solution)/shard_map/while/body/eval_jaxpr/dynamic_update_slice | solution.py:114
  104.3 3.9 add_bitcast_fusion.4
  111.5 6.2 %dynamic_update_slice.13 = f32[2,384,768]{2,1,0:T(8,128)} dynamic-update-slice(f32[2,384,768]{2,1,0:T(8,128)} %get-tuple-element.624, f32[2,256,256]{2,1,0:T(8,128)S(1)} %get-tuple-element.602, s32[]{:T(128)} %constant.167.clone.1..sunk, s32[]{:T(128)S(6)} %select_n.153, s32[]{:T(128)S(6)} %select_n.154) | dynamic-update-slice | bytes 1048580 | tf_op jit(solution)/shard_map/while/body/eval_jaxpr/dynamic_update_slice | solution.py:114
  143.0 3.9 add_bitcast_fusion.4
  150.1 6.1 %dynamic_update_slice.13 = f32[2,384,768]{2,1,0:T(8,128)} dynamic-update-slice(f32[2,384,768]{2,1,0:T(8,128)} %get-tuple-element.624, f32[2,256,256]{2,1,0:T(8,128)S(1)} %get-tuple-element.602, s32[]{:T(128)} %constant.167.clone.1..sunk, s32[]{:T(128)S(6)} %select_n.153, s32[]{:T(128)S(6)} %select_n.154) | dynamic-update-slice | bytes 1048580 | tf_op jit(solution)/shard_map/while/body/eval_jaxpr/dynamic_update_slice | solution.py:114
  181.4 3.9 add_bitcast_fusion.4
  188.6 6.2 %dynamic_update_slice.13 = f32[2,384,768]{2,1,0:T(8,128)} dynamic-update-slice(f32[2,384,768]{2,1,0:T(8,128)} %get-tuple-element.624, f32[2,256,256]{2,1,0:T(8,128)S(1)} %get-tuple-element.602, s32[]{:T(128)} %constant.167.clone.1..sunk, s32[]{:T(128)S(6)} %select_n.153, s32[]{:T(128)S(6)} %select_n.154) | dynamic-update-slice | bytes 1048580 | tf_op jit(solution)/shard_map/while/body/eval_jaxpr/dynamic_update_slice | solution.py:114
  220.0 3.9 add_bitcast_fusion.4
  227.1 6.3 %dynamic_update_slice.13 = f32[2,384,768]{2,1,0:T(8,128)} dynamic-update-slice(f32[2,384,768]{2,1,0:T(8,128)} %get-tuple-element.624, f32[2,256,256]{2,1,0:T(8,128)S(1)} %get-tuple-element.602, s32[]{:T(128)} %constant.167.clone.1..sunk, s32[]{:T(128)S(6)} %select_n.153, s32[]{:T(128)S(6)} %select_n.154) | dynamic-update-slice | bytes 1048580 | tf_op jit(solution)/shard_map/while/body/eval_jaxpr/dynamic_update_slice | solution.py:114
  258.7 3.9 add_bitcast_fusion.4
  265.8 6.3 %dynamic_update_slice.13 = f32[2,384,768]{2,1,0:T(8,128)} dynamic-update-slice(f32[2,384,768]{2,1,0:T(8,128)} %get-tuple-element.624, f32[2,256,256]{2,1,0:T(8,128)S(1)} %get-tuple-element.602, s32[]{:T(128)} %constant.167.clone.1..sunk, s32[]{:T(128)S(6)} %select_n.153, s32[]{:T(128)S(6)} %select_n.154) | dynamic-update-slice | bytes 1048580 | tf_op jit(solution)/shard_map/while/body/eval_jaxpr/dynamic_update_slice | solution.py:114
  290.9 24.8 %all_to_all.14 = f32[16,1,1024]{2,1,0:T(1,128)S(1)} all-to-all(f32[16,1,1024]{2,1,0:T(1,128)S(1)} %reshape.143), channel_id=1, replica_groups=mesh['tile'=4,'proj'=16,'cuts'=4] {'proj'}, dimensions={0} | all-to-all | bytes 131072 | tf_op jit(solution)/shard_map/all_to_all | solution.py:10
  318.2 3.3 all-to-all-start.1
  322.8 3.7 all-to-all-done.1
  327.6 121.8 %reduce-scatter.4.cloned.1.call-done = f32[32,512]{1,0:T(8,128)} async-done(((f32[2048,512]{1,0:T(8,128)}), f32[32,512]{1,0:T(8,128)}) %reduce-scatter.4.cloned.1.call-update) | async-done | bytes 65552
  451.2 128.4 %all-reduce.3.cloned.1.call-done = f32[131200]{0:T(1024)} async-done(((f32[131200]{0:T(1024)}), f32[131200]{0:T(1024)}) %all-reduce.3.cloned.1.call-update) | async-done | bytes 524816 | tf_op jit(solution)/shard_map/psum | solution.py:137
  590.8 3.8 fusion.116
  594.7 4.7 convolution_subtract_fusion.4
  (209 shorter events, 188.6 us)
Async XLA Ops:
  8.0 18.8 %copy-start = (bf16[16,32,2048]{2,1,0:T(8,128)(2,1)S(1)}, bf16[16,32,2048]{2,1,0:T(8,128)(2,1)}, u32[]{:S(2)}) copy-start(bf16[16,32,2048]{2,1,0:T(8,128)(2,1)} %param.25) | copy-start | bytes 6291460
  8.0 441.4 %reduce-scatter.4.cloned.1.call-start = ((), (), s32[]{:S(2)}) async-start(), calls=%async_computation.5 | async-start | bytes 4259840
  8.1 11.9 %copy-start.3 = (f32[8,32,2048]{2,1,0:T(8,128)S(1)}, f32[8,32,2048]{2,1,0:T(8,128)}, u32[]{:S(2)}) copy-start(f32[8,32,2048]{2,1,0:T(8,128)} %param.24) | copy-start | bytes 6291460
  10.3 26.2 %collective-permute-start.1 = (f32[2,384,128]{2,1,0:T(8,128)}, f32[2,384,128]{2,1,0:T(8,128)S(1)}, u32[]{:S(2)}, u32[]{:S(2)}) collective-permute-start(f32[2,384,128]{2,1,0:T(8,128)} %get-tuple-element.513), channel_id=1, source_target_pairs={{64,0},{128,64},{192,128},{65,1},{129,65},{193,129},{66,2},{130,66... | collective-permute-start | bytes 1179656 | tf_op jit(solution)/shard_map/ppermute | solution.py:18
  11.6 24.9 %collective-permute-start = (f32[2,384,128]{2,1,0:T(8,128)}, f32[2,384,128]{2,1,0:T(8,128)}, u32[]{:S(2)}, u32[]{:S(2)}) collective-permute-start(f32[2,384,128]{2,1,0:T(8,128)} %get-tuple-element.512), channel_id=1, source_target_pairs={{0,64},{64,128},{128,192},{1,65},{65,129},{129,193},{2,66},{66,130... | collective-permute-start | bytes 1179656 | tf_op jit(solution)/shard_map/ppermute | solution.py:18
  19.1 0.8 copy-start.6
  35.4 1.0 copy-start.4
  39.6 1.6 copy-start.11
  39.6 1.6 copy-start.12
  274.9 10.6 %collective-permute-start.2 = (f32[2,384,128]{2,1,0:T(8,128)}, f32[2,384,128]{2,1,0:T(8,128)S(1)}, u32[]{:S(2)}, u32[]{:S(2)}) collective-permute-start(f32[2,384,128]{2,1,0:T(8,128)} %get-tuple-element.511), channel_id=1, source_target_pairs={{0,64},{64,128},{128,192},{1,65},{65,129},{129,193},{2,66},{66,130... | collective-permute-start | bytes 1179656 | tf_op jit(solution)/shard_map/ppermute | solution.py:18
  278.0 10.1 %collective-permute-start.3 = (f32[2,384,128]{2,1,0:T(8,128)S(1)}, f32[2,384,128]{2,1,0:T(8,128)S(1)}, u32[]{:S(2)}, u32[]{:S(2)}) collective-permute-start(f32[2,384,128]{2,1,0:T(8,128)S(1)} %get-tuple-element.510), channel_id=1, source_target_pairs={{64,0},{128,64},{192,128},{65,1},{129,65},{193,129},{66,2},{130,66... | collective-permute-start | bytes 1179656 | tf_op jit(solution)/shard_map/ppermute | solution.py:18
  281.7 6.6 %copy-start.2 = (f32[1,2,384,512]{3,2,1,0:T(8,128)S(1)}, f32[1,2,384,512]{3,2,1,0:T(8,128)}, u32[]{:S(2)}) copy-start(f32[1,2,384,512]{3,2,1,0:T(8,128)} %param.17) | copy-start | bytes 4718596
  288.3 1.6 copy-start.9
  288.7 1.1 copy-start.8
  289.8 31.7 %copy-start.1 = (f32[2,256,256]{2,1,0:T(8,128)S(1)}, f32[2,256,256]{2,1,0:T(8,128)}, u32[]{:S(2)}) copy-start(f32[2,256,256]{2,1,0:T(8,128)} %get-tuple-element.383) | copy-start | bytes 1572868
  318.2 8.3 %all-to-all-start.1 = ((f32[4,1,4096]{2,1,0:T(1,128)}), f32[4,1,4096]{2,1,0:T(1,128)S(1)}, u32[]{:S(2)}, u32[]{:S(2)}) async-start(f32[4,1,4096]{2,1,0:T(1,128)} %reshape.145), calls=%async_computation.1 | async-start | bytes 131072 | tf_op jit(solution)/shard_map/all_to_all | solution.py:146
  321.5 258.1 %all-reduce.3.cloned.1.call-start = ((), (), s32[]{:S(2)}) async-start(), calls=%async_computation.3 | async-start | bytes 1056768 | tf_op jit(solution)/shard_map/psum | solution.py:137
  321.9 129.3 %copy-start.10 = (s32[64]{0:T(128)S(1)}, s32[64]{0:T(128)}, u32[]{:S(2)}) copy-start(s32[64]{0:T(128)} %param.27) | copy-start | bytes 772
  322.7 262.6 %all-gather.2.cloned.1.call-start = ((), (), s32[]{:S(2)}) async-start(), calls=%async_computation.4 | async-start | bytes 2129920 | tf_op jit(solution)/shard_map/all_gather | solution.py:180
  327.3 257.2 %copy-start.5 = (f32[2,256,256]{2,1,0:T(8,128)S(1)}, f32[2,256,256]{2,1,0:T(8,128)}, u32[]{:S(2)}) copy-start(f32[2,256,256]{2,1,0:T(8,128)} %param.18) | copy-start | bytes 1572868
  590.8 4.0 copy-start.7
Sparse Core Ops, SparseCore 0:
  35.6 413.7 reduce-scatter.3
  452.9 85.0 all-gather.1
Sparse Core Ops, SparseCore 1:
  328.1 251.4 all-reduce.2
